TPU v7x, 32 devices: a whole 2x2x4 slice. The times are simulated.
32 devices in a mesh: tower: 2 (over y), dp: 16 (over z, x, core).
Axes of the slice: x: 2, y: 2, z: 4, core: 2. Of those that a mesh axis runs over, the one named last changes fastest.
Arguments:
- tokens: bfloat16 [2, 4096, 768], P('tower', 'dp'), may hold values from -6 to 6
- query_lengths: int32 [64], P('dp'), may hold values from 8 to 64, as said below
- doc_lengths: int32 [16], P('dp'), may hold values from 32 to 256, as said below
- positives: int32 [64], replicated, may hold values from 0 to 15
- w_qkv: bfloat16 [768, 2304], P('dp'), may hold values from -0.21875 to 0.21875
- w_out: bfloat16 [768, 768], P('dp'), may hold values from -0.21875 to 0.21875
- w_gate: bfloat16 [768, 3072], P('dp'), may hold values from -0.21875 to 0.21875
- w_up: bfloat16 [768, 3072], P('dp'), may hold values from -0.21875 to 0.21875
- w_down: bfloat16 [3072, 768], P('dp'), may hold values from -0.109375 to 0.109375
- ln1_gain: bfloat16 [768], P('dp'), may hold values from 0.5 to 1.5
- first_layernorm_shift: bfloat16 [768], P('dp'), may hold values from -0.59765625 to 0.59765625
- ln2_gain: bfloat16 [768], P('dp'), may hold values from 0.5 to 1.5
- ln2_bias: bfloat16 [768], P('dp'), may hold values from -0.6 to 0.6
Outputs:
- loss: float32 [], replicated
- query_embeddings: float32 [64, 768], P('dp')
- doc_embeddings: float32 [16, 768], P('dp')
- token_grad: float32 [2, 4096, 768], P('tower', 'dp')
- w_qkv_grad: float32 [768, 2304], P('dp')
- w_out_grad: float32 [768, 768], P('dp')
- w_gate_grad: float32 [768, 3072], P('dp')
- w_up_grad: float32 [768, 3072], P('dp')
- w_down_grad: float32 [3072, 768], P('dp')
- ln1_gain_grad: float32 [768], P('dp')
- ln1_bias_grad: float32 [768], P('dp')
- ln2_gain_grad: float32 [768], P('dp')
- ln2_bias_grad: float32 [768], P('dp')
Inputs may be any that keep to these rules, and one draw needn't show every extreme that they name: `query_lengths`: each query has 8 to 64 real tokens in the first slots of its block; some query has 64. `doc_lengths`: each document has 32 to 256 real tokens in the first slots; some document has 256.
All inputs are finite; a program needn't handle non-finite values.
Results may differ from a plain program's by a relative error of at most 0.0085.
Values may be sent and summed in bfloat16 or wider, within the bound.
A program may use at most 128 MiB of HBM per device.

v0:
```python
import jax
import jax.numpy as jnp
from jax import lax
from jax.sharding import PartitionSpec as P

D = 768
HEADS = 12
HEAD = 64
QLEN = 64
QPD = 4
exact_product_accuracy = lax.Precision.HIGHEST
rope_base = 1000.0
contrast_sharpness_factor = 0.02


def product(left, right):
    return jnp.dot(left, right, preferred_element_type=jnp.float32)


def rotary_tables(places):
    freqs = jnp.power(rope_base, -2.0 * jnp.arange(HEAD // 2).astype(jnp.float32) / HEAD)
    angles = places[:, None] * freqs[None, :]
    return (jnp.cos(angles)[:, None, :], jnp.sin(angles)[:, None, :])


def rotate(values, cosines, sines):
    half_dim = values.shape[-1] // 2
    first = values[..., :half_dim]
    second = values[..., half_dim:]
    return jnp.concatenate(
        [first * cosines - second * sines, second * cosines + first * sines], axis=-1
    )


def layer_norm(hidden, gain, offset):
    average = jnp.mean(hidden, -1, keepdims=True)
    centred = hidden - average
    variance = jnp.mean(centred * centred, -1, keepdims=True)
    return centred * lax.rsqrt(variance + 1e-05) * gain + offset


def normalize(pooled):
    return pooled * lax.rsqrt(jnp.sum(pooled * pooled, -1, keepdims=True) + 1e-06)


def layout(tower_id, query_len, doc_len, count):
    places = jnp.arange(count)
    span = jnp.where(tower_id == 0, QLEN, count)
    segment = places // span
    offset_in = places - segment * span
    slots = jnp.arange(QPD)
    seg_limit = jnp.where(tower_id == 0, query_len, doc_len[0] * jnp.ones_like(query_len))
    limit = jnp.sum(jnp.where(segment[:, None] == slots[None, :], seg_limit[None, :], 0), axis=1)
    valid = offset_in < limit
    allowed = (segment[:, None] == segment[None, :]) & valid[None, :]
    member = (segment[None, :] == slots[:, None]) & valid[None, :]
    pool_matrix = jnp.where(member, 1.0 / seg_limit[:, None].astype(jnp.float32), 0.0)
    return (offset_in.astype(jnp.float32), allowed, pool_matrix)


def swish_product(left, right):
    return jax.nn.silu(left) * right


def on_device(
    tokens,
    query_lengths,
    doc_lengths,
    positives,
    w_qkv,
    w_out,
    w_gate,
    w_up,
    w_down,
    ln1_gain,
    first_layernorm_shift,
    ln2_gain,
    ln2_bias,
):
    tower_id = lax.axis_index("tower")
    device_id = lax.axis_index("dp")
    groups = lax.axis_size("dp")
    full = (
        lax.all_gather(w_qkv, "dp", axis=0, tiled=True),
        lax.all_gather(w_out, "dp", axis=0, tiled=True),
        lax.all_gather(w_gate, "dp", axis=0, tiled=True),
        lax.all_gather(w_up, "dp", axis=0, tiled=True),
        lax.all_gather(w_down, "dp", axis=0, tiled=True),
        lax.all_gather(ln1_gain, "dp", axis=0, tiled=True),
        lax.all_gather(first_layernorm_shift, "dp", axis=0, tiled=True),
        lax.all_gather(ln2_gain, "dp", axis=0, tiled=True),
        lax.all_gather(ln2_bias, "dp", axis=0, tiled=True),
    )
    qkv_full, out_full, gate_full, up_full, down_full = (
        full[0],
        full[1],
        full[2],
        full[3],
        full[4],
    )
    gain_one = full[5].astype(jnp.float32)
    bias_one = full[6].astype(jnp.float32)
    gain_two = full[7].astype(jnp.float32)
    bias_two = full[8].astype(jnp.float32)
    inputs = tokens[0]
    count = inputs.shape[0]
    places, allowed, pool_matrix = layout(tower_id, query_lengths, doc_lengths, count)
    cosines, sines = rotary_tables(places)
    packed = product(inputs, qkv_full)
    raw_query = packed[:, :D].reshape(count, HEADS, HEAD)
    raw_key = packed[:, D : 2 * D].reshape(count, HEADS, HEAD)

    def rotate_both(first, second):
        return (rotate(first, cosines, sines), rotate(second, cosines, sines))

    rotated, rotary_back = jax.vjp(rotate_both, raw_query, raw_key)
    query_low = rotated[0].astype(jnp.bfloat16)
    key_low = rotated[1].astype(jnp.bfloat16)
    value_low = packed[:, 2 * D :].reshape(count, HEADS, HEAD).astype(jnp.bfloat16)
    scale = HEAD ** (-0.5)

    def masked_scores():
        scores = (
            jnp.einsum("ihd,jhd->hij", query_low, key_low, preferred_element_type=jnp.float32)
            * scale
        )
        return jnp.where(allowed[None], scores, -1e30)

    scores = masked_scores()
    peak = jnp.max(scores, -1, keepdims=True)
    log_total = peak + jnp.log(jnp.sum(jnp.exp(scores - peak), -1, keepdims=True))
    probs_low = jnp.exp(scores - log_total).astype(jnp.bfloat16)
    mixed = jnp.einsum("hij,jhd->ihd", probs_low, value_low, preferred_element_type=jnp.float32)
    mixed_low = mixed.reshape(count, D).astype(jnp.bfloat16)
    attended = product(mixed_low, out_full)
    inputs_wide = inputs.astype(jnp.float32)
    normed_one, norm_one_back = jax.vjp(layer_norm, inputs_wide + attended, gain_one, bias_one)
    feed = normed_one.astype(jnp.bfloat16)
    gate = product(feed, gate_full)
    up_part = product(feed, up_full)
    hidden_wide, swish_back = jax.vjp(swish_product, gate, up_part)
    hidden = hidden_wide.astype(jnp.bfloat16)
    branch = product(hidden, down_full)
    normed_two, norm_two_back = jax.vjp(layer_norm, normed_one + branch, gain_two, bias_two)
    pooled = jnp.dot(pool_matrix, normed_two, precision=exact_product_accuracy)
    embedded, normal_back = jax.vjp(normalize, pooled)
    gathered = lax.all_gather(embedded, ("tower", "dp"), axis=0, tiled=True)
    queries_total = groups * QPD
    gathered_query_rows = gathered[:queries_total]
    gathered_document_rows = gathered[queries_total:].reshape(groups, QPD, D)[:, 0]
    pairwise_affinity_matrix = (
        jnp.dot(gathered_query_rows, gathered_document_rows.T, precision=exact_product_accuracy)
        / contrast_sharpness_factor
    )
    peak_logit = jnp.max(pairwise_affinity_matrix, -1, keepdims=True)
    log_partition_norm = peak_logit + jnp.log(
        jnp.sum(jnp.exp(pairwise_affinity_matrix - peak_logit), -1, keepdims=True)
    )
    columns = lax.broadcasted_iota(jnp.int32, pairwise_affinity_matrix.shape, 1)
    matching_labels = columns == positives[:, None]
    picked = jnp.sum(jnp.where(matching_labels, pairwise_affinity_matrix, 0.0), -1, keepdims=True)
    total = jnp.sum(log_partition_norm - picked)
    loss = total / queries_total
    similarity_gradient = (
        jnp.exp(pairwise_affinity_matrix - log_partition_norm) - matching_labels.astype(jnp.float32)
    ) / contrast_sharpness_factor
    own_rows = lax.dynamic_slice_in_dim(similarity_gradient, device_id * QPD, QPD, 0)
    query_side = jnp.dot(own_rows, gathered_document_rows, precision=exact_product_accuracy)
    own_column = lax.dynamic_slice_in_dim(similarity_gradient, device_id, 1, 1)
    doc_side = jnp.dot(own_column.T, gathered_query_rows, precision=exact_product_accuracy)
    doc_side = jnp.concatenate([doc_side, jnp.zeros((QPD - 1, D), jnp.float32)], 0)
    embed_grad = jnp.where(tower_id == 0, query_side, doc_side)
    pooled_grad = normal_back(embed_grad)[0]
    top_grad = jnp.dot(pool_matrix.T, pooled_grad, precision=exact_product_accuracy)
    sum_two, gain_two_grad, bias_two_grad = norm_two_back(top_grad)
    attention_input_cotangent, out_back, gate_back, up_back, down_back = (
        qkv_full,
        out_full,
        gate_full,
        up_full,
        down_full,
    )
    branch_low = sum_two.astype(jnp.bfloat16)
    down_grad = product(hidden.T, branch_low)
    hidden_grad = product(branch_low, down_back.T)
    gate_grad_wide, up_grad_wide = swish_back(hidden_grad)
    gate_low = gate_grad_wide.astype(jnp.bfloat16)
    up_low = up_grad_wide.astype(jnp.bfloat16)
    gate_weight_grad = product(feed.T, gate_low)
    up_weight_grad = product(feed.T, up_low)
    feed_grad = sum_two + product(gate_low, gate_back.T) + product(up_low, up_back.T)
    sum_one, gain_one_grad, bias_one_grad = norm_one_back(feed_grad)
    attend_low = sum_one.astype(jnp.bfloat16)
    out_grad = product(mixed_low.T, attend_low)
    mixed_grad = product(attend_low, out_back.T).astype(jnp.bfloat16).reshape(count, HEADS, HEAD)
    probs_again = jnp.exp(masked_scores() - log_total)
    prob_grad = jnp.einsum(
        "ihd,jhd->hij", mixed_grad, value_low, preferred_element_type=jnp.float32
    )
    score_grad = probs_again * (prob_grad - jnp.sum(probs_again * prob_grad, -1, keepdims=True))
    score_low = score_grad.astype(jnp.bfloat16)
    query_grad = (
        jnp.einsum("hij,jhd->ihd", score_low, key_low, preferred_element_type=jnp.float32) * scale
    )
    key_grad = (
        jnp.einsum("hij,ihd->jhd", score_low, query_low, preferred_element_type=jnp.float32) * scale
    )
    value_grad = jnp.einsum(
        "hij,ihd->jhd",
        probs_again.astype(jnp.bfloat16),
        mixed_grad,
        preferred_element_type=jnp.float32,
    )
    raw_query_grad, raw_key_grad = rotary_back((query_grad, key_grad))
    packed_grad = jnp.concatenate(
        [
            raw_query_grad.reshape(count, D),
            raw_key_grad.reshape(count, D),
            value_grad.reshape(count, D),
        ],
        1,
    ).astype(jnp.bfloat16)
    qkv_grad = product(inputs.T, packed_grad)
    input_grad = sum_one + product(packed_grad, attention_input_cotangent.T)
    gradients = (
        qkv_grad,
        out_grad,
        gate_weight_grad,
        up_weight_grad,
        down_grad,
        gain_one_grad,
        bias_one_grad,
        gain_two_grad,
        bias_two_grad,
    )
    partial_sums = (
        lax.psum_scatter(gradients[0], "dp", scatter_dimension=0, tiled=True),
        lax.psum_scatter(gradients[1], "dp", scatter_dimension=0, tiled=True),
        lax.psum_scatter(gradients[2], "dp", scatter_dimension=0, tiled=True),
        lax.psum_scatter(gradients[3], "dp", scatter_dimension=0, tiled=True),
        lax.psum_scatter(gradients[4], "dp", scatter_dimension=0, tiled=True),
        lax.psum_scatter(gradients[5], "dp", scatter_dimension=0, tiled=True),
        lax.psum_scatter(gradients[6], "dp", scatter_dimension=0, tiled=True),
        lax.psum_scatter(gradients[7], "dp", scatter_dimension=0, tiled=True),
        lax.psum_scatter(gradients[8], "dp", scatter_dimension=0, tiled=True),
    )
    tower_halves = (
        lax.psum_scatter(
            partial_sums[0].astype(jnp.bfloat16), "tower", scatter_dimension=0, tiled=True
        ).astype(jnp.float32),
        lax.psum_scatter(
            partial_sums[1].astype(jnp.bfloat16), "tower", scatter_dimension=0, tiled=True
        ).astype(jnp.float32),
        lax.psum_scatter(
            partial_sums[2].astype(jnp.bfloat16), "tower", scatter_dimension=0, tiled=True
        ).astype(jnp.float32),
        lax.psum_scatter(
            partial_sums[3].astype(jnp.bfloat16), "tower", scatter_dimension=0, tiled=True
        ).astype(jnp.float32),
        lax.psum_scatter(
            partial_sums[4].astype(jnp.bfloat16), "tower", scatter_dimension=0, tiled=True
        ).astype(jnp.float32),
        lax.psum_scatter(
            partial_sums[5].astype(jnp.bfloat16), "tower", scatter_dimension=0, tiled=True
        ).astype(jnp.float32),
        lax.psum_scatter(
            partial_sums[6].astype(jnp.bfloat16), "tower", scatter_dimension=0, tiled=True
        ).astype(jnp.float32),
        lax.psum_scatter(
            partial_sums[7].astype(jnp.bfloat16), "tower", scatter_dimension=0, tiled=True
        ).astype(jnp.float32),
        lax.psum_scatter(
            partial_sums[8].astype(jnp.bfloat16), "tower", scatter_dimension=0, tiled=True
        ).astype(jnp.float32),
    )
    shares = (
        lax.all_gather(tower_halves[0].astype(jnp.bfloat16), "tower", axis=0, tiled=True).astype(
            jnp.float32
        ),
        lax.all_gather(tower_halves[1].astype(jnp.bfloat16), "tower", axis=0, tiled=True).astype(
            jnp.float32
        ),
        lax.all_gather(tower_halves[2].astype(jnp.bfloat16), "tower", axis=0, tiled=True).astype(
            jnp.float32
        ),
        lax.all_gather(tower_halves[3].astype(jnp.bfloat16), "tower", axis=0, tiled=True).astype(
            jnp.float32
        ),
        lax.all_gather(tower_halves[4].astype(jnp.bfloat16), "tower", axis=0, tiled=True).astype(
            jnp.float32
        ),
        lax.all_gather(tower_halves[5].astype(jnp.bfloat16), "tower", axis=0, tiled=True).astype(
            jnp.float32
        ),
        lax.all_gather(tower_halves[6].astype(jnp.bfloat16), "tower", axis=0, tiled=True).astype(
            jnp.float32
        ),
        lax.all_gather(tower_halves[7].astype(jnp.bfloat16), "tower", axis=0, tiled=True).astype(
            jnp.float32
        ),
        lax.all_gather(tower_halves[8].astype(jnp.bfloat16), "tower", axis=0, tiled=True).astype(
            jnp.float32
        ),
    )
    query_rows = lax.dynamic_slice_in_dim(gathered_query_rows, device_id * QPD, QPD, 0)
    doc_row = lax.dynamic_slice_in_dim(gathered_document_rows, device_id, 1, 0)
    return (loss, query_rows, doc_row, input_grad[None]) + tuple(shares)


def solution(mesh):
    return jax.shard_map(
        on_device,
        mesh=mesh,
        in_specs=(
            P("tower", "dp", None),
            P("dp"),
            P("dp"),
            P(),
            P("dp", None),
            P("dp", None),
            P("dp", None),
            P("dp", None),
            P("dp", None),
            P("dp"),
            P("dp"),
            P("dp"),
            P("dp"),
        ),
        out_specs=(
            P(),
            P("dp", None),
            P("dp", None),
            P("tower", "dp", None),
            P("dp", None),
            P("dp", None),
            P("dp", None),
            P("dp", None),
            P("dp", None),
            P("dp"),
            P("dp"),
            P("dp"),
            P("dp"),
        ),
        check_vma=False,
    )
```

profile of v0, /device:TPU:0, one launch (start us, length us, event | category | flops | bytes accessed | tf_op | source)
XLA Modules:
  0.0 923.1 jit_solution(9459486310065083493)
XLA Ops:
  11.3 1.3 fusion.71
  16.6 35.8 %all-reduce.22 = (bf16[768]{0:T(1024)(128)(2,1)S(1)}, bf16[768]{0:T(1024)(128)(2,1)S(1)}, bf16[768]{0:T(1024)(128)(2,1)S(1)}, bf16[768]{0:T(1024)(128)(2,1)S(1)}) all-reduce(bf16[768]{0:T(1024)(128)(2,1)S(1)} %dynamic-update-slice.1, bf16[768]{0:T(1024)(128)(2,1)S(1)} %dynamic-update-slice, ...), channel_id=1, replica_groups=mesh['tower'=2,'dp'=16] {'dp'}, use_global_device_ids=true, to_apply=%add.6 | all-reduce | flops 3072 | bytes 12288
  55.1 1.2 convert_divide_fusion
  57.2 3.2 all-gather.7.cloned.1.call-done
  60.4 3.2 fusion.16
  65.6 1.4 copy.58
  68.4 1.5 exponential_reduce_fusion
  70.0 1.6 convolution_convert_fusion.2
  71.6 28.5 %all-gather.9.cloned.1.call-done = bf16[768,768]{1,0:T(8,128)(2,1)} async-done(((bf16[48,768]{1,0:T(8,128)(2,1)}), bf16[768,768]{1,0:T(8,128)(2,1)}) %all-gather.9.cloned.1.call-update) | async-done | bytes 1179664 | tf_op jit(solution)/shard_map/all_gather | solution.py:85
  100.1 2.0 fusion.73
  103.8 50.9 %all-gather.11.cloned.1.call-done = bf16[768,3072]{1,0:T(8,128)(2,1)} async-done(((bf16[48,3072]{1,0:T(8,128)(2,1)}), bf16[768,3072]{1,0:T(8,128)(2,1)}) %all-gather.11.cloned.1.call-update) | async-done | bytes 4718608 | tf_op jit(solution)/shard_map/all_gather | solution.py:86
  154.6 5.3 fusion.76
  160.0 48.6 %all-gather.13.cloned.1.call-done = bf16[768,3072]{1,0:T(8,128)(2,1)} async-done(((bf16[48,3072]{1,0:T(8,128)(2,1)}), bf16[768,3072]{1,0:T(8,128)(2,1)}) %all-gather.13.cloned.1.call-update) | async-done | bytes 4718608 | tf_op jit(solution)/shard_map/all_gather | solution.py:87
  208.6 7.2 multiply_convert_fusion.2
  215.8 46.8 %all-gather.15.cloned.1.call-done = bf16[3072,768]{1,0:T(8,128)(2,1)} async-done(((bf16[192,768]{1,0:T(8,128)(2,1)}), bf16[3072,768]{1,0:T(8,128)(2,1)}) %all-gather.15.cloned.1.call-update) | async-done | bytes 4718608 | tf_op jit(solution)/shard_map/all_gather | solution.py:88
  262.6 4.6 fusion.74
  269.5 40.3 %all-gather = f32[32,4,768]{2,1,0:T(4,128)S(1)} all-gather(f32[1,4,768]{2,1,0:T(4,128)S(1)} %multiply_bitcast_fusion), channel_id=1, replica_groups=mesh['tower'=2,'dp'=16] {'tower','dp'}, dimensions={0}, use_global_device_ids=true | all-gather | bytes 405504 | tf_op jit(solution)/shard_map/all_gather | solution.py:147
  311.2 1.7 reshape.352
  312.8 1.4 fusion.75
  316.2 1.1 fusion.53
  317.4 1.2 multiply_reduce_fusion.7
  319.2 2.9 multiply_reduce_fusion.1
  322.7 1.6 fusion.69
  324.4 7.6 multiply_convert_fusion.1
  332.2 1.6 convolution_add_fusion.3
  333.9 2.3 multiply_reduce_fusion.2
  337.5 1.9 fusion.67
  339.7 2.8 convolution_convert_fusion.1
  342.5 1.9 copy.61
  344.4 2.2 multiply_reduce_fusion
  351.3 3.9 convolution_bitcast_fusion
  355.3 8.1 copy.70
  363.4 1.5 copy-done.20
  364.9 5.0 fusion.77
  370.1 1.3 copy-done.18
  371.4 5.1 fusion.78
  376.6 1.1 copy-done.8
  378.1 5.1 fusion.65
  383.5 15.4 %reduce-scatter.15.cloned.1.call-done = f32[48,768]{1,0:T(8,128)} async-done(((f32[768,768]{1,0:T(8,128)}), f32[48,768]{1,0:T(8,128)}) %reduce-scatter.15.cloned.1.call-update) | async-done | bytes 147472 | tf_op jit(solution)/shard_map/reduce_scatter | solution.py:238
  398.9 1.6 convert_element_type.176
  400.5 92.0 %reduce-scatter.31.cloned.1.call-done = f32[48,2304]{1,0:T(8,128)} async-done(((f32[768,2304]{1,0:T(8,128)}), f32[48,2304]{1,0:T(8,128)}) %reduce-scatter.31.cloned.1.call-update) | async-done | bytes 442384
  492.5 1.3 copy.71
  494.9 112.7 %reduce-scatter.19.cloned.1.call-done = f32[48,3072]{1,0:T(8,128)} async-done(((f32[768,3072]{1,0:T(8,128)}), f32[48,3072]{1,0:T(8,128)}) %reduce-scatter.19.cloned.1.call-update) | async-done | bytes 589840 | tf_op jit(solution)/shard_map/reduce_scatter | solution.py:239
  607.5 1.8 convert_element_type.178
  609.4 113.9 %reduce-scatter.23.cloned.1.call-done = f32[48,3072]{1,0:T(8,128)} async-done(((f32[768,3072]{1,0:T(8,128)}), f32[48,3072]{1,0:T(8,128)}) %reduce-scatter.23.cloned.1.call-update) | async-done | bytes 589840 | tf_op jit(solution)/shard_map/reduce_scatter | solution.py:240
  723.3 1.8 convert_element_type.180
  727.2 62.3 %all-reduce.21 = (bf16[768]{0:T(1024)(128)(2,1)S(1)}, bf16[768]{0:T(1024)(128)(2,1)S(1)}, bf16[768]{0:T(1024)(128)(2,1)S(1)}, bf16[768]{0:T(1024)(128)(2,1)S(1)}) all-reduce(f32[768]{0:T(1024)S(1)} %copy-done.63, f32[768]{0:T(1024)S(1)} %copy-done.64, f32[768]{0:T(1024)S(1)} %copy-done.48, ...), channel_id=12, replica_groups=mesh['tower'=2,'dp'=16] {'dp'}, use_global_device_ids=true, to_apply=%region_29.30.clone | all-reduce | flops 3072 | bytes 18432
  789.8 5.2 all-reduce.24
  796.1 4.9 all-reduce.23
  803.8 1.3 dynamic-slice_bitcast_fusion
  805.0 1.3 constant_dynamic-slice_fusion
  806.4 32.3 %reduce-scatter.27.cloned.1.call-done = f32[192,768]{1,0:T(8,128)} async-done(((f32[3072,768]{1,0:T(8,128)}), f32[192,768]{1,0:T(8,128)}) %reduce-scatter.27.cloned.1.call-update) | async-done | bytes 589840 | tf_op jit(solution)/shard_map/reduce_scatter | solution.py:241
  838.7 1.8 convert_element_type.182
  840.6 4.0 fusion.8
  844.6 6.7 reduce-scatter.17.cloned.1.call-done
  851.3 4.8 all_gather.68
  856.8 7.9 reduce-scatter.33.cloned.1.call-done
  864.7 5.7 all_gather.67
  871.1 8.5 reduce-scatter.21.cloned.1.call-done
  879.6 6.5 all_gather.69
  886.9 6.9 reduce-scatter.25.cloned.1.call-done
  893.9 6.5 all_gather.70
  901.2 6.9 reduce-scatter.29.cloned.1.call-done
  908.1 6.5 all_gather.71
  (255 shorter events, 37.7 us)
Async XLA Ops:
  7.2 53.2 %all-gather.7.cloned.1.call-start = ((), (), s32[]{:S(2)}) async-start(), calls=%async_computation.10 | async-start | bytes 3760128 | tf_op jit(solution)/shard_map/all_gather | solution.py:84
  7.9 92.2 %all-gather.9.cloned.1.call-start = ((), (), s32[]{:S(2)}) async-start(), calls=%async_computation.11 | async-start | bytes 1253376 | tf_op jit(solution)/shard_map/all_gather | solution.py:85
  8.7 146.0 %all-gather.11.cloned.1.call-start = ((), (), s32[]{:S(2)}) async-start(), calls=%async_computation.12 | async-start | bytes 5013504 | tf_op jit(solution)/shard_map/all_gather | solution.py:86
  9.4 199.2 %all-gather.13.cloned.1.call-start = ((), (), s32[]{:S(2)}) async-start(), calls=%async_computation.13 | async-start | bytes 5013504 | tf_op jit(solution)/shard_map/all_gather | solution.py:87
  10.0 252.6 %all-gather.15.cloned.1.call-start = ((), (), s32[]{:S(2)}) async-start(), calls=%async_computation.14 | async-start | bytes 5013504 | tf_op jit(solution)/shard_map/all_gather | solution.py:88
  10.6 388.3 %reduce-scatter.15.cloned.1.call-start = ((), (), s32[]{:S(2)}) async-start(), calls=%async_computation.15 | async-start | bytes 2506752 | tf_op jit(solution)/shard_map/reduce_scatter | solution.py:238
  55.0 1.7 copy-start.42
  57.0 10.2 %copy-start.34 = (f32[256,32]{0,1:T(8,128)}, f32[256,32]{0,1:T(8,128)S(1)}, u32[]{:S(2)}) copy-start(f32[256,32]{0,1:T(8,128)S(1)} %get-tuple-element.87) | copy-start | bytes 98308
  57.0 10.2 %copy-start.36 = (f32[256,32]{0,1:T(8,128)}, f32[256,32]{0,1:T(8,128)S(1)}, u32[]{:S(2)}) copy-start(f32[256,32]{0,1:T(8,128)S(1)} %get-tuple-element.88) | copy-start | bytes 98308
  57.2 10.4 %copy-start.21 = (pred[256,256]{0,1:T(8,128)(4,1)}, pred[256,256]{0,1:T(8,128)(4,1)S(1)}, u32[]{:S(2)}) copy-start(pred[256,256]{0,1:T(8,128)(4,1)S(1)} %compare_and_fusion) | copy-start | bytes 196612
  67.6 2.4 copy-start.14
  68.3 1.7 copy-start.22
  68.4 31.7 %copy-start.5 = (bf16[1,256,768]{2,1,0:T(8,128)(2,1)S(1)}, bf16[1,256,768]{2,1,0:T(8,128)(2,1)}, u32[]{:S(2)}) copy-start(bf16[1,256,768]{2,1,0:T(8,128)(2,1)} %param.13) | copy-start | bytes 1179652
  100.1 3.4 copy-start.39
  100.1 3.4 copy-start.47
  262.5 5.5 copy-start.41
  262.5 5.5 copy-start.43
  262.6 5.5 copy-start.59
  262.6 5.5 copy-start.62
  262.6 5.5 copy-start.65
  267.2 42.7 %copy-start.46 = (f32[256]{0:T(256)}, f32[256]{0:T(256)S(1)}, u32[]{:S(2)}) copy-start(f32[256]{0:T(256)S(1)} %broadcast_multiply_fusion) | copy-start | bytes 3076
  267.9 42.6 %copy-start.52 = (f32[256]{0:T(256)}, f32[256]{0:T(256)S(1)}, u32[]{:S(2)}) copy-start(f32[256]{0:T(256)S(1)} %fusion.50) | copy-start | bytes 3076
  268.8 41.7 %copy-start.67 = (f32[4]{0:T(128)}, f32[4]{0:T(128)S(1)}, u32[]{:S(2)}) copy-start(f32[4]{0:T(128)S(1)} %get-tuple-element.101) | copy-start | bytes 52
  312.8 11.6 %copy-start.68 = (f32[256,3072]{1,0:T(8,128)S(1)}, f32[256,3072]{1,0:T(8,128)}, u32[]{:S(2)}) copy-start(f32[256,3072]{1,0:T(8,128)} %fusion.76) | copy-start | bytes 9437188
  322.7 9.4 %slice-start = ((s8[4718592]{0:T(1024)(128)(4,1)}), s8[4194304]{0:T(1024)(128)(4,1)S(1)}, s32[]{:S(2)}) async-start(s8[4718592]{0:T(1024)(128)(4,1)} %bitcast.92), calls=%async_computation.25 | async-start | bytes 8388608
  322.7 11.0 %slice-start.2 = ((s8[4718592]{0:T(1024)(128)(4,1)}), s8[4194304]{0:T(1024)(128)(4,1)S(1)}, s32[]{:S(2)}) async-start(s8[4718592]{0:T(1024)(128)(4,1)} %bitcast.94), calls=%async_computation.27 | async-start | bytes 8388608
  324.4 7.7 copy-start.7
  324.4 7.7 copy-start.60
  324.4 7.7 slice-start.1
  324.4 9.4 %slice-start.3 = ((s8[4718592]{0:T(1024)(128)(4,1)}), s8[524288]{0:T(1024)(128)(4,1)S(1)}, s32[]{:S(2)}) async-start(s8[4718592]{0:T(1024)(128)(4,1)} %bitcast.94), calls=%async_computation.28 | async-start | bytes 1048576
  332.1 1.7 copy-start.19
  332.1 1.7 copy-start.17
  332.1 1.7 copy-start.1
  332.1 1.7 copy-start.40
  332.2 1.7 copy-start.45
  332.2 1.7 copy-start.51
  333.9 2.4 copy-start.54
  333.9 3.6 copy-start.16
  339.4 153.1 %reduce-scatter.31.cloned.1.call-start = ((), (), s32[]{:S(2)}) async-start(), calls=%async_computation.23 | async-start | bytes 7520256
  344.4 2.3 copy-start.23
  346.7 1.4 copy-start.25
  346.7 1.4 copy-start.27
  349.1 1.5 copy-start.10
  349.1 2.3 copy-start.6
  363.4 1.6 copy-start.20
  363.4 244.1 %reduce-scatter.19.cloned.1.call-start = ((), (), s32[]{:S(2)}) async-start(), calls=%async_computation.17 | async-start | bytes 10027008 | tf_op jit(solution)/shard_map/reduce_scatter | solution.py:239
  370.0 353.3 %reduce-scatter.23.cloned.1.call-start = ((), (), s32[]{:S(2)}) async-start(), calls=%async_computation.19 | async-start | bytes 10027008 | tf_op jit(solution)/shard_map/reduce_scatter | solution.py:240
  376.5 1.7 copy-start.9
  376.5 1.7 copy-start.61
  376.5 462.2 %reduce-scatter.27.cloned.1.call-start = ((), (), s32[]{:S(2)}) async-start(), calls=%async_computation.21 | async-start | bytes 10027008 | tf_op jit(solution)/shard_map/reduce_scatter | solution.py:241
  383.3 343.8 %copy-start.48 = (f32[768]{0:T(1024)S(1)}, f32[768]{0:T(1024)}, u32[]{:S(2)}) copy-start(f32[768]{0:T(1024)} %get-tuple-element.39) | copy-start | bytes 9220
  383.3 343.8 %copy-start.49 = (f32[768]{0:T(1024)S(1)}, f32[768]{0:T(1024)}, u32[]{:S(2)}) copy-start(f32[768]{0:T(1024)} %get-tuple-element.43) | copy-start | bytes 9220
  383.3 343.8 %copy-start.63 = (f32[768]{0:T(1024)S(1)}, f32[768]{0:T(1024)}, u32[]{:S(2)}) copy-start(f32[768]{0:T(1024)} %get-tuple-element.41) | copy-start | bytes 9220
  383.3 343.8 %copy-start.64 = (f32[768]{0:T(1024)S(1)}, f32[768]{0:T(1024)}, u32[]{:S(2)}) copy-start(f32[768]{0:T(1024)} %get-tuple-element.44) | copy-start | bytes 9220
  383.4 457.1 %copy-start.4 = (f32[256,768]{1,0:T(8,128)S(1)}, f32[256,768]{1,0:T(8,128)}, u32[]{:S(2)}) copy-start(f32[256,768]{1,0:T(8,128)} %copy-done.3) | copy-start | bytes 2359300
  383.4 457.1 %copy-start.11 = (bf16[256,12,64]{0,2,1:T(8,128)(2,1)S(1)}, bf16[256,12,64]{0,2,1:T(8,128)(2,1)}, u32[]{:S(2)}) copy-start(bf16[256,12,64]{0,2,1:T(8,128)(2,1)} %copy-done.10) | copy-start | bytes 1179652
  383.4 457.1 %copy-start.13 = (bf16[256,12,64]{0,2,1:T(8,128)(2,1)S(1)}, bf16[256,12,64]{0,2,1:T(8,128)(2,1)}, u32[]{:S(2)}) copy-start(bf16[256,12,64]{0,2,1:T(8,128)(2,1)} %copy-done.12) | copy-start | bytes 1179652
  383.4 457.1 %copy-start.33 = (bf16[12,64,256]{2,1,0:T(8,128)(2,1)S(1)}, bf16[12,64,256]{2,1,0:T(8,128)(2,1)}, u32[]{:S(2)}) copy-start(bf16[12,64,256]{2,1,0:T(8,128)(2,1)} %copy-done.32) | copy-start | bytes 1179652
  383.4 457.1 %copy-start.57 = (f32[256]{0:T(256)S(1)}, f32[256]{0:T(256)}, u32[]{:S(2)}) copy-start(f32[256]{0:T(256)} %copy-done.56) | copy-start | bytes 3076
  383.4 467.8 %reduce-scatter.17.cloned.1.call-start = ((), (), s32[]{:S(2)}) async-start(), calls=%async_computation.16 | async-start | bytes 110592 | tf_op jit(solution)/shard_map/reduce_scatter | solution.py:251
  400.4 464.2 %reduce-scatter.33.cloned.1.call-start = ((), (), s32[]{:S(2)}) async-start(), calls=%async_computation.24 | async-start | bytes 331776 | tf_op jit(solution)/shard_map/reduce_scatter | solution.py:248
  494.8 384.8 %reduce-scatter.21.cloned.1.call-start = ((), (), s32[]{:S(2)}) async-start(), calls=%async_computation.18 | async-start | bytes 442368 | tf_op jit(solution)/shard_map/reduce_scatter | solution.py:254
  609.4 284.5 %reduce-scatter.25.cloned.1.call-start = ((), (), s32[]{:S(2)}) async-start(), calls=%async_computation.20 | async-start | bytes 442368 | tf_op jit(solution)/shard_map/reduce_scatter | solution.py:257
  725.2 182.9 %reduce-scatter.29.cloned.1.call-start = ((), (), s32[]{:S(2)}) async-start(), calls=%async_computation.22 | async-start | bytes 442368 | tf_op jit(solution)/shard_map/reduce_scatter | solution.py:260
  (24 other events, 20.1 us)
Sparse Core Ops, SparseCore 0:
  10.3 50.0 all-gather.6
  62.7 37.4 all-gather.8
  102.4 52.1 all-gather.10
  156.8 51.7 all-gather.12
  210.7 51.7 all-gather.14
  339.5 59.2 reduce-scatter.14
  403.4 89.0 reduce-scatter.30
  496.6 110.8 reduce-scatter.18
  612.2 111.1 reduce-scatter.22
  727.3 111.3 reduce-scatter.26
  841.5 9.6 reduce-scatter.16
  853.4 11.1 reduce-scatter.32
  867.6 12.0 reduce-scatter.20
  881.8 12.0 reduce-scatter.24
  896.0 12.0 reduce-scatter.28
where the time goes:
time: 924 us; the launch traced here: 923 us
  waiting for transfers between devices  585 us (63%)
  blocking collectives  178 us (19%)
  matrix products  75.5 us (8%)
  local copies, waits for them, and re-layouts  37.5 us (4%)
  other arithmetic  26.3 us (3%)
  between operations  20 us (2%)
    reduce_scatter x1, waiting for transfers between devices, on_device(): lax.psum_scatter(gradients[3], 'dp', scatter_dimension=0, tiled=True)  114 us
    reduce_scatter x1, waiting for transfers between devices, on_device(): lax.psum_scatter(gradients[2], 'dp', scatter_dimension=0, tiled=True)  113 us
    unnamed x4, blocking collectives  108 us
    unnamed x16, waiting for transfers between devices  95.3 us
    dot_general x15, matrix products, product(): return jnp.dot(left, right, preferred_element_type=jnp.float32)  61.8 us
    all_gather x1, waiting for transfers between devices, on_device(): lax.all_gather(w_gate, 'dp', axis=0, tiled=True)  50.9 us
    all_gather x1, waiting for transfers between devices, on_device(): lax.all_gather(w_up, 'dp', axis=0, tiled=True)  48.6 us
    all_gather x1, waiting for transfers between devices, on_device(): lax.all_gather(w_down, 'dp', axis=0, tiled=True)  46.8 us
  transfers between devices with their start and end apart: 15, of which 15 were waited for; matrix products, arithmetic and copies ran while one was open for 10% of the time, Pallas kernels for 0%

commit v1 on v0

--- a/solution.py
+++ b/solution.py
@@ -1,3 +1,4 @@
+import functools
 import jax
 import jax.numpy as jnp
 from jax import lax
@@ -11,6 +12,43 @@
 exact_product_accuracy = lax.Precision.HIGHEST
 rope_base = 1000.0
 contrast_sharpness_factor = 0.02
+
+
+def _return_all_marks(patch, dim_at):
+    r1 = list(patch.shape[1:])
+    r1[dim_at] *= patch.shape[0]
+    moved = jnp.moveaxis(patch, 0, dim_at).reshape(r1)
+    return moved
+
+
+def place_the_sectors(piece_in, which_axis, dim_k):
+    many = lax.psum(1, axis_name=which_axis)
+    samples = []
+    for dev in range(many):
+        samples.append((dev, (dev + 1) % many))
+    column = []
+    for jj, tick in samples:
+        column.append((tick, jj))
+    a_next, row_out = ([], [])
+    for idx in range(many - 1):
+        if idx % 2 == 0:
+            a_next.append(
+                lax.ppermute(a_next[-1] if a_next else piece_in, axis_name=which_axis, perm=samples)
+            )
+        else:
+            row_out.append(
+                lax.ppermute(
+                    row_out[-1] if row_out else piece_in, axis_name=which_axis, perm=column
+                )
+            )
+    kept_arr = jnp.stack([*a_next[::-1], piece_in, *row_out], axis=0)
+    passed = lax.axis_index(which_axis) - len(a_next)
+    kept_arr = kept_arr[(jnp.arange(many) - passed) % many]
+    extra = _return_all_marks(kept_arr, dim_k)
+    return extra
+
+
+feed_the_strings = functools.partial(place_the_sectors, which_axis="dp", dim_k=0)
 
 
 def product(left, right):
@@ -83,7 +121,7 @@
     full = (
         lax.all_gather(w_qkv, "dp", axis=0, tiled=True),
         lax.all_gather(w_out, "dp", axis=0, tiled=True),
-        lax.all_gather(w_gate, "dp", axis=0, tiled=True),
+        feed_the_strings(w_gate),
         lax.all_gather(w_up, "dp", axis=0, tiled=True),
         lax.all_gather(w_down, "dp", axis=0, tiled=True),
         lax.all_gather(ln1_gain, "dp", axis=0, tiled=True),

time: 924 us -> 883 us (0.956)
  waiting for transfers between devices: 585 us -> 497 us
  starting transfers between devices: 0.82 us -> 29.4 us
  local copies, waits for them, and re-layouts: 37.5 us -> 54.9 us
    all_gather x1 -> x0, waiting for transfers between devices: 50.9 us -> none  [on_device(): lax.all_gather(w_gate, 'dp', axis=0, tiled=True)]
    all_gather x1, waiting for transfers between devices: 48.6 us -> 5.59 us  [on_device(): lax.all_gather(w_up, 'dp', axis=0, tiled=True)]
    ppermute x0 -> x15, waiting for transfers between devices: none -> 37.7 us  [the longest x8 23.9 us: place_the_sectors(): lax.ppermute(a_next[-1] if a_next else piece_in, axis_name=which_axis, pe...]
    ppermute x0 -> x15, starting transfers between devices: none -> 28.6 us  [the longest x7 27.5 us: place_the_sectors(): lax.ppermute(row_out[-1] if row_out else piece_in, axis_name=which_axis,...]
    all_gather x1, waiting for transfers between devices: 28.5 us -> 0.01 us  [on_device(): lax.all_gather(w_out, 'dp', axis=0, tiled=True)]
    unnamed x174 -> x189, local copies, waits for them, and re-layouts: 26.4 us -> 37.6 us
    unnamed x16 -> x15, waiting for transfers between devices: 95.3 us -> 94.2 us
  transfers between devices with their start and end apart: 15 -> 29, of which waited for: 15 -> 23; matrix products, arithmetic and copies ran while one was open for 10% -> 13% of each run, Pallas kernels for 0% -> 0%
where the time goes in v1:
time: 883 us; the launch traced here: 882 us
  waiting for transfers between devices  497 us (56%)
  blocking collectives  178 us (20%)
  matrix products  76.4 us (9%)
  local copies, waits for them, and re-layouts  54.9 us (6%)
  starting transfers between devices  29.4 us (3%)
  other arithmetic  26.8 us (3%)
  between operations  20 us (2%)
    reduce_scatter x1, waiting for transfers between devices, on_device(): lax.psum_scatter(gradients[3], 'dp', scatter_dimension=0, tiled=True)  114 us
    reduce_scatter x1, waiting for transfers between devices, on_device(): lax.psum_scatter(gradients[2], 'dp', scatter_dimension=0, tiled=True)  113 us
    unnamed x4, blocking collectives  107 us
    unnamed x15, waiting for transfers between devices  94.2 us
    dot_general x15, matrix products, product(): return jnp.dot(left, right, preferred_element_type=jnp.float32)  61.8 us
    all_gather x1, waiting for transfers between devices, on_device(): lax.all_gather(w_down, 'dp', axis=0, tiled=True)  46.9 us
    all_gather x1, blocking collectives, on_device(): gathered = lax.all_gather(embedded, ('tower', 'dp'), axis=0, tiled=True)  40.3 us
    unnamed x189, local copies, waits for them, and re-layouts  37.6 us
  transfers between devices with their start and end apart: 29, of which 23 were waited for; matrix products, arithmetic and copies ran while one was open for 13% of the time, Pallas kernels for 0%

profile of v1, /device:TPU:0, one launch (start us, length us, event | category | flops | bytes accessed | tf_op | source)
XLA Modules:
  0.0 881.9 jit_solution(12851647384505985561)
XLA Ops:
  10.0 9.6 %collective-permute-done = bf16[48,3072]{1,0:T(8,128)(2,1)S(1)} collective-permute-done((bf16[48,3072]{1,0:T(8,128)(2,1)}, bf16[48,3072]{1,0:T(8,128)(2,1)S(1)}, u32[]{:S(2)}, u32[]{:S(2)}) %collective-permute-start) | collective-permute-done | bytes 294944 | tf_op jit(solution)/shard_map/ppermute | solution.py:36
  19.5 4.4 collective-permute-start.8
  24.0 8.0 collective-permute-done.1
  32.0 4.4 collective-permute-start.9
  36.4 4.4 collective-permute-done.2
  46.9 34.9 %all-reduce.22 = (bf16[768]{0:T(1024)(128)(2,1)S(1)}, bf16[768]{0:T(1024)(128)(2,1)S(1)}, bf16[768]{0:T(1024)(128)(2,1)S(1)}, bf16[768]{0:T(1024)(128)(2,1)S(1)}) all-reduce(bf16[768]{0:T(1024)(128)(2,1)S(1)} %dynamic-update-slice.1, bf16[768]{0:T(1024)(128)(2,1)S(1)} %dynamic-update-slice, ...), channel_id=1, replica_groups=mesh['tower'=2,'dp'=16] {'dp'}, use_global_device_ids=true, to_apply=%add.6 | all-reduce | flops 3072 | bytes 12288
  86.3 2.5 collective-permute-done.10
  88.8 4.7 collective-permute-start.11
  93.8 5.5 collective-permute-done.11
  99.3 4.6 collective-permute-start.12
  105.3 2.9 collective-permute-done.12
  108.2 4.7 collective-permute-start.13
  114.2 2.9 collective-permute-done.13
  117.1 4.6 collective-permute-start.14
  134.2 5.5 gather_fusion
  139.7 3.2 fusion.16
  147.5 1.6 fusion.4
  149.8 1.6 convolution_convert_fusion.2
  151.5 2.0 fusion.75
  154.9 5.5 fusion.78
  160.4 5.6 all-gather.10.cloned.1.call-done
  166.0 7.1 multiply_convert_fusion.2
  173.2 46.9 %all-gather.12.cloned.1.call-done = bf16[3072,768]{1,0:T(8,128)(2,1)} async-done(((bf16[192,768]{1,0:T(8,128)(2,1)}), bf16[3072,768]{1,0:T(8,128)(2,1)}) %all-gather.12.cloned.1.call-update) | async-done | bytes 4718608 | tf_op jit(solution)/shard_map/all_gather | solution.py:126
  220.1 4.6 fusion.76
  227.0 40.3 %all-gather = f32[32,4,768]{2,1,0:T(4,128)S(1)} all-gather(f32[1,4,768]{2,1,0:T(4,128)S(1)} %multiply_bitcast_fusion), channel_id=1, replica_groups=mesh['tower'=2,'dp'=16] {'tower','dp'}, dimensions={0}, use_global_device_ids=true | all-gather | bytes 405504 | tf_op jit(solution)/shard_map/all_gather | solution.py:185
  268.7 1.7 reshape.413
  276.8 2.9 multiply_reduce_fusion.1
  280.3 1.6 fusion.71
  282.0 7.6 multiply_convert_fusion.1
  289.8 1.4 convolution_add_fusion.3
  291.5 2.3 multiply_reduce_fusion.2
  295.1 1.9 fusion.69
  297.4 2.8 convolution_convert_fusion.1
  300.2 1.9 copy.61
  302.1 2.2 multiply_reduce_fusion
  309.0 3.9 convolution_bitcast_fusion
  312.9 8.0 copy.70
  321.0 1.5 copy-done.20
  322.6 5.1 fusion.79
  329.0 5.1 fusion.80
  335.8 5.2 fusion.67
  341.1 15.4 %reduce-scatter.15.cloned.1.call-done = f32[48,768]{1,0:T(8,128)} async-done(((f32[768,768]{1,0:T(8,128)}), f32[48,768]{1,0:T(8,128)}) %reduce-scatter.15.cloned.1.call-update) | async-done | bytes 147472 | tf_op jit(solution)/shard_map/reduce_scatter | solution.py:276
  356.5 1.6 convert_element_type.176
  358.1 91.9 %reduce-scatter.31.cloned.1.call-done = f32[48,2304]{1,0:T(8,128)} async-done(((f32[768,2304]{1,0:T(8,128)}), f32[48,2304]{1,0:T(8,128)}) %reduce-scatter.31.cloned.1.call-update) | async-done | bytes 442384
  452.3 112.7 %reduce-scatter.19.cloned.1.call-done = f32[48,3072]{1,0:T(8,128)} async-done(((f32[768,3072]{1,0:T(8,128)}), f32[48,3072]{1,0:T(8,128)}) %reduce-scatter.19.cloned.1.call-update) | async-done | bytes 589840 | tf_op jit(solution)/shard_map/reduce_scatter | solution.py:277
  565.0 1.8 convert_element_type.178
  566.9 113.9 %reduce-scatter.23.cloned.1.call-done = f32[48,3072]{1,0:T(8,128)} async-done(((f32[768,3072]{1,0:T(8,128)}), f32[48,3072]{1,0:T(8,128)}) %reduce-scatter.23.cloned.1.call-update) | async-done | bytes 589840 | tf_op jit(solution)/shard_map/reduce_scatter | solution.py:278
  680.8 1.8 convert_element_type.180
  684.7 62.3 %all-reduce.21 = (bf16[768]{0:T(1024)(128)(2,1)S(1)}, bf16[768]{0:T(1024)(128)(2,1)S(1)}, bf16[768]{0:T(1024)(128)(2,1)S(1)}, bf16[768]{0:T(1024)(128)(2,1)S(1)}) all-reduce(f32[768]{0:T(1024)S(1)} %copy-done.63, f32[768]{0:T(1024)S(1)} %copy-done.64, f32[768]{0:T(1024)S(1)} %copy-done.48, ...), channel_id=12, replica_groups=mesh['tower'=2,'dp'=16] {'dp'}, use_global_device_ids=true, to_apply=%region_29.30.clone | all-reduce | flops 3072 | bytes 18432
  747.3 5.2 all-reduce.24
  753.7 4.9 all-reduce.23
  763.9 33.6 %reduce-scatter.27.cloned.1.call-done = f32[192,768]{1,0:T(8,128)} async-done(((f32[3072,768]{1,0:T(8,128)}), f32[192,768]{1,0:T(8,128)}) %reduce-scatter.27.cloned.1.call-update) | async-done | bytes 589840 | tf_op jit(solution)/shard_map/reduce_scatter | solution.py:279
  797.5 1.8 convert_element_type.182
  799.4 4.0 fusion.8
  803.4 6.5 reduce-scatter.17.cloned.1.call-done
  810.0 4.8 all_gather.64
  815.5 8.1 reduce-scatter.33.cloned.1.call-done
  823.5 5.7 all_gather.63
  830.0 8.4 reduce-scatter.21.cloned.1.call-done
  838.4 6.4 all_gather.65
  845.7 7.1 reduce-scatter.25.cloned.1.call-done
  852.7 6.4 all_gather.66
  860.0 6.9 reduce-scatter.29.cloned.1.call-done
  867.0 6.4 all_gather.67
  (301 shorter events, 66.8 us)
Async XLA Ops:
  7.2 121.2 %copy-start.37 = (bf16[48,3072]{1,0:T(8,128)(2,1)S(1)}, bf16[48,3072]{1,0:T(8,128)(2,1)}, u32[]{:S(2)}) copy-start(bf16[48,3072]{1,0:T(8,128)(2,1)} %param.19) | copy-start | bytes 884740
  7.2 132.5 %all-gather.6.cloned.1.call-start = ((), (), s32[]{:S(2)}) async-start(), calls=%async_computation.10 | async-start | bytes 3760128 | tf_op jit(solution)/shard_map/all_gather | solution.py:122
  7.9 143.5 %all-gather.8.cloned.1.call-start = ((), (), s32[]{:S(2)}) async-start(), calls=%async_computation.11 | async-start | bytes 1253376 | tf_op jit(solution)/shard_map/all_gather | solution.py:123
  8.7 157.4 %all-gather.10.cloned.1.call-start = ((), (), s32[]{:S(2)}) async-start(), calls=%async_computation.12 | async-start | bytes 5013504 | tf_op jit(solution)/shard_map/all_gather | solution.py:125
  9.4 210.6 %all-gather.12.cloned.1.call-start = ((), (), s32[]{:S(2)}) async-start(), calls=%async_computation.13 | async-start | bytes 5013504 | tf_op jit(solution)/shard_map/all_gather | solution.py:126
  9.5 10.1 %collective-permute-start = (bf16[48,3072]{1,0:T(8,128)(2,1)}, bf16[48,3072]{1,0:T(8,128)(2,1)S(1)}, u32[]{:S(2)}, u32[]{:S(2)}) collective-permute-start(bf16[48,3072]{1,0:T(8,128)(2,1)} %param.19), channel_id=1, source_target_pairs={{0,1},{1,2},{2,3},{3,4},{4,5},{5,6},{6,7},{7,8},{8,9},{9,10},{10,1... | collective-permute-start | bytes 884744 | tf_op jit(solution)/shard_map/ppermute | solution.py:36
  19.5 12.5 %collective-permute-start.1 = (bf16[48,3072]{1,0:T(8,128)(2,1)S(1)}, bf16[48,3072]{1,0:T(8,128)(2,1)S(1)}, u32[]{:S(2)}, u32[]{:S(2)}) collective-permute-start(bf16[48,3072]{1,0:T(8,128)(2,1)S(1)} %collective-permute-done), channel_id=1, source_target_pairs={{0,1},{1,2},{2,3},{3,4},{4,5},{5,6},{6,7},{7,8},{8,9},{9,10},{10,1... | collective-permute-start | bytes 884744 | tf_op jit(solution)/shard_map/ppermute | solution.py:36
  19.5 12.5 %collective-permute-start.8 = (bf16[48,3072]{1,0:T(8,128)(2,1)}, bf16[48,3072]{1,0:T(8,128)(2,1)S(1)}, u32[]{:S(2)}, u32[]{:S(2)}) collective-permute-start(bf16[48,3072]{1,0:T(8,128)(2,1)} %param.19), channel_id=1, source_target_pairs={{1,0},{2,1},{3,2},{4,3},{5,4},{6,5},{7,6},{8,7},{9,8},{10,9},{11,1... | collective-permute-start | bytes 884744 | tf_op jit(solution)/shard_map/ppermute | solution.py:40
  32.0 8.8 %collective-permute-start.2 = (bf16[48,3072]{1,0:T(8,128)(2,1)S(1)}, bf16[48,3072]{1,0:T(8,128)(2,1)S(1)}, u32[]{:S(2)}, u32[]{:S(2)}) collective-permute-start(bf16[48,3072]{1,0:T(8,128)(2,1)S(1)} %collective-permute-done.1), channel_id=1, source_target_pairs={{0,1},{1,2},{2,3},{3,4},{4,5},{5,6},{6,7},{7,8},{8,9},{9,10},{10,1... | collective-permute-start | bytes 884744 | tf_op jit(solution)/shard_map/ppermute | solution.py:36
  32.0 52.5 %collective-permute-start.9 = (bf16[48,3072]{1,0:T(8,128)(2,1)S(1)}, bf16[48,3072]{1,0:T(8,128)(2,1)S(1)}, u32[]{:S(2)}, u32[]{:S(2)}) collective-permute-start(bf16[48,3072]{1,0:T(8,128)(2,1)S(1)} %collective-permute-done.8), channel_id=1, source_target_pairs={{1,0},{2,1},{3,2},{4,3},{5,4},{6,5},{7,6},{8,7},{9,8},{10,9},{11,1... | collective-permute-start | bytes 884744 | tf_op jit(solution)/shard_map/ppermute | solution.py:40
  40.8 43.8 %collective-permute-start.3 = (bf16[48,3072]{1,0:T(8,128)(2,1)S(1)}, bf16[48,3072]{1,0:T(8,128)(2,1)S(1)}, u32[]{:S(2)}, u32[]{:S(2)}) collective-permute-start(bf16[48,3072]{1,0:T(8,128)(2,1)S(1)} %collective-permute-done.2), channel_id=1, source_target_pairs={{0,1},{1,2},{2,3},{3,4},{4,5},{5,6},{6,7},{7,8},{8,9},{9,10},{10,1... | collective-permute-start | bytes 884744 | tf_op jit(solution)/shard_map/ppermute | solution.py:36
  40.9 315.6 %reduce-scatter.15.cloned.1.call-start = ((), (), s32[]{:S(2)}) async-start(), calls=%async_computation.14 | async-start | bytes 2506752 | tf_op jit(solution)/shard_map/reduce_scatter | solution.py:276
  84.4 29.8 %copy-start.42 = (s32[256]{0:T(256)}, s32[256]{0:T(256)S(1)}, u32[]{:S(2)}) copy-start(s32[256]{0:T(256)S(1)} %and_select_fusion.1) | copy-start | bytes 3076
  84.5 4.3 collective-permute-start.10
  84.6 9.0 %collective-permute-start.4 = (bf16[48,3072]{1,0:T(8,128)(2,1)S(1)}, bf16[48,3072]{1,0:T(8,128)(2,1)S(1)}, u32[]{:S(2)}, u32[]{:S(2)}) collective-permute-start(bf16[48,3072]{1,0:T(8,128)(2,1)S(1)} %collective-permute-done.3), channel_id=1, source_target_pairs={{0,1},{1,2},{2,3},{3,4},{4,5},{5,6},{6,7},{7,8},{8,9},{9,10},{10,1... | collective-permute-start | bytes 884744 | tf_op jit(solution)/shard_map/ppermute | solution.py:36
  88.8 10.4 %collective-permute-start.11 = (bf16[48,3072]{1,0:T(8,128)(2,1)S(1)}, bf16[48,3072]{1,0:T(8,128)(2,1)S(1)}, u32[]{:S(2)}, u32[]{:S(2)}) collective-permute-start(bf16[48,3072]{1,0:T(8,128)(2,1)S(1)} %collective-permute-done.10), channel_id=1, source_target_pairs={{1,0},{2,1},{3,2},{4,3},{5,4},{6,5},{7,6},{8,7},{9,8},{10,9},{11,1... | collective-permute-start | bytes 884744 | tf_op jit(solution)/shard_map/ppermute | solution.py:40
  93.6 10.9 %collective-permute-start.5 = (bf16[48,3072]{1,0:T(8,128)(2,1)S(1)}, bf16[48,3072]{1,0:T(8,128)(2,1)S(1)}, u32[]{:S(2)}, u32[]{:S(2)}) collective-permute-start(bf16[48,3072]{1,0:T(8,128)(2,1)S(1)} %collective-permute-done.4), channel_id=1, source_target_pairs={{0,1},{1,2},{2,3},{3,4},{4,5},{5,6},{6,7},{7,8},{8,9},{9,10},{10,1... | collective-permute-start | bytes 884744 | tf_op jit(solution)/shard_map/ppermute | solution.py:36
  93.7 20.5 %copy-start.58 = (pred[256]{0:T(512)(128)(4,1)}, pred[256]{0:T(512)(128)(4,1)S(1)}, u32[]{:S(2)}) copy-start(pred[256]{0:T(512)(128)(4,1)S(1)} %fusion.48) | copy-start | bytes 772
  99.3 9.0 %collective-permute-start.12 = (bf16[48,3072]{1,0:T(8,128)(2,1)S(1)}, bf16[48,3072]{1,0:T(8,128)(2,1)S(1)}, u32[]{:S(2)}, u32[]{:S(2)}) collective-permute-start(bf16[48,3072]{1,0:T(8,128)(2,1)S(1)} %collective-permute-done.11), channel_id=1, source_target_pairs={{1,0},{2,1},{3,2},{4,3},{5,4},{6,5},{7,6},{8,7},{9,8},{10,9},{11,1... | collective-permute-start | bytes 884744 | tf_op jit(solution)/shard_map/ppermute | solution.py:40
  104.5 8.9 %collective-permute-start.6 = (bf16[48,3072]{1,0:T(8,128)(2,1)S(1)}, bf16[48,3072]{1,0:T(8,128)(2,1)S(1)}, u32[]{:S(2)}, u32[]{:S(2)}) collective-permute-start(bf16[48,3072]{1,0:T(8,128)(2,1)S(1)} %collective-permute-done.5), channel_id=1, source_target_pairs={{0,1},{1,2},{2,3},{3,4},{4,5},{5,6},{6,7},{7,8},{8,9},{9,10},{10,1... | collective-permute-start | bytes 884744 | tf_op jit(solution)/shard_map/ppermute | solution.py:36
  108.2 8.9 %collective-permute-start.13 = (bf16[48,3072]{1,0:T(8,128)(2,1)S(1)}, bf16[48,3072]{1,0:T(8,128)(2,1)S(1)}, u32[]{:S(2)}, u32[]{:S(2)}) collective-permute-start(bf16[48,3072]{1,0:T(8,128)(2,1)S(1)} %collective-permute-done.12), channel_id=1, source_target_pairs={{1,0},{2,1},{3,2},{4,3},{5,4},{6,5},{7,6},{8,7},{9,8},{10,9},{11,1... | collective-permute-start | bytes 884744 | tf_op jit(solution)/shard_map/ppermute | solution.py:40
  113.4 9.0 %collective-permute-start.7 = (bf16[48,3072]{1,0:T(8,128)(2,1)S(1)}, bf16[48,3072]{1,0:T(8,128)(2,1)S(1)}, u32[]{:S(2)}, u32[]{:S(2)}) collective-permute-start(bf16[48,3072]{1,0:T(8,128)(2,1)S(1)} %collective-permute-done.6), channel_id=1, source_target_pairs={{0,1},{1,2},{2,3},{3,4},{4,5},{5,6},{6,7},{7,8},{8,9},{9,10},{10,1... | collective-permute-start | bytes 884744 | tf_op jit(solution)/shard_map/ppermute | solution.py:36
  117.1 16.4 %collective-permute-start.14 = (bf16[48,3072]{1,0:T(8,128)(2,1)S(1)}, bf16[48,3072]{1,0:T(8,128)(2,1)S(1)}, u32[]{:S(2)}, u32[]{:S(2)}) collective-permute-start(bf16[48,3072]{1,0:T(8,128)(2,1)S(1)} %collective-permute-done.13), channel_id=1, source_target_pairs={{1,0},{2,1},{3,2},{4,3},{5,4},{6,5},{7,6},{8,7},{9,8},{10,9},{11,1... | collective-permute-start | bytes 884744 | tf_op jit(solution)/shard_map/ppermute | solution.py:40
  134.2 5.5 copy-start.5
  146.6 2.6 copy-start.21
  147.5 2.3 copy-start.14
  151.4 2.9 copy-start.39
  151.4 2.9 copy-start.47
  220.1 5.5 copy-start.41
  220.1 5.5 copy-start.43
  220.1 5.5 copy-start.59
  220.1 5.5 copy-start.62
  220.1 5.5 copy-start.65
  224.7 42.7 %copy-start.46 = (f32[256]{0:T(256)}, f32[256]{0:T(256)S(1)}, u32[]{:S(2)}) copy-start(f32[256]{0:T(256)S(1)} %broadcast_multiply_fusion) | copy-start | bytes 3076
  225.5 42.6 %copy-start.52 = (f32[256]{0:T(256)}, f32[256]{0:T(256)S(1)}, u32[]{:S(2)}) copy-start(f32[256]{0:T(256)S(1)} %fusion.50) | copy-start | bytes 3076
  226.4 41.7 %copy-start.67 = (f32[4]{0:T(128)}, f32[4]{0:T(128)S(1)}, u32[]{:S(2)}) copy-start(f32[4]{0:T(128)S(1)} %get-tuple-element.101) | copy-start | bytes 52
  270.4 11.6 %copy-start.68 = (f32[256,3072]{1,0:T(8,128)S(1)}, f32[256,3072]{1,0:T(8,128)}, u32[]{:S(2)}) copy-start(f32[256,3072]{1,0:T(8,128)} %fusion.78) | copy-start | bytes 9437188
  280.3 9.4 %slice-start = ((s8[4718592]{0:T(1024)(128)(4,1)}), s8[4194304]{0:T(1024)(128)(4,1)S(1)}, s32[]{:S(2)}) async-start(s8[4718592]{0:T(1024)(128)(4,1)} %bitcast.114), calls=%async_computation.24 | async-start | bytes 8388608
  280.3 11.1 %slice-start.2 = ((s8[4718592]{0:T(1024)(128)(4,1)}), s8[4194304]{0:T(1024)(128)(4,1)S(1)}, s32[]{:S(2)}) async-start(s8[4718592]{0:T(1024)(128)(4,1)} %bitcast.131), calls=%async_computation.26 | async-start | bytes 8388608
  282.0 7.7 copy-start.7
  282.0 7.7 copy-start.60
  282.0 7.7 slice-start.1
  282.0 9.4 %slice-start.3 = ((s8[4718592]{0:T(1024)(128)(4,1)}), s8[524288]{0:T(1024)(128)(4,1)S(1)}, s32[]{:S(2)}) async-start(s8[4718592]{0:T(1024)(128)(4,1)} %bitcast.131), calls=%async_computation.27 | async-start | bytes 1048576
  291.5 2.4 copy-start.54
  291.5 3.6 copy-start.16
  297.1 153.0 %reduce-scatter.31.cloned.1.call-start = ((), (), s32[]{:S(2)}) async-start(), calls=%async_computation.22 | async-start | bytes 7520256
  306.7 2.3 copy-start.6
  321.0 244.1 %reduce-scatter.19.cloned.1.call-start = ((), (), s32[]{:S(2)}) async-start(), calls=%async_computation.16 | async-start | bytes 10027008 | tf_op jit(solution)/shard_map/reduce_scatter | solution.py:277
  327.7 353.2 %reduce-scatter.23.cloned.1.call-start = ((), (), s32[]{:S(2)}) async-start(), calls=%async_computation.18 | async-start | bytes 10027008 | tf_op jit(solution)/shard_map/reduce_scatter | solution.py:278
  334.1 463.4 %reduce-scatter.27.cloned.1.call-start = ((), (), s32[]{:S(2)}) async-start(), calls=%async_computation.20 | async-start | bytes 10027008 | tf_op jit(solution)/shard_map/reduce_scatter | solution.py:279
  341.0 343.7 %copy-start.48 = (f32[768]{0:T(1024)S(1)}, f32[768]{0:T(1024)}, u32[]{:S(2)}) copy-start(f32[768]{0:T(1024)} %get-tuple-element.39) | copy-start | bytes 9220
  341.0 343.7 %copy-start.49 = (f32[768]{0:T(1024)S(1)}, f32[768]{0:T(1024)}, u32[]{:S(2)}) copy-start(f32[768]{0:T(1024)} %get-tuple-element.43) | copy-start | bytes 9220
  341.0 343.7 %copy-start.63 = (f32[768]{0:T(1024)S(1)}, f32[768]{0:T(1024)}, u32[]{:S(2)}) copy-start(f32[768]{0:T(1024)} %get-tuple-element.41) | copy-start | bytes 9220
  341.0 343.7 %copy-start.64 = (f32[768]{0:T(1024)S(1)}, f32[768]{0:T(1024)}, u32[]{:S(2)}) copy-start(f32[768]{0:T(1024)} %get-tuple-element.44) | copy-start | bytes 9220
  341.0 458.4 %copy-start.4 = (f32[256,768]{1,0:T(8,128)S(1)}, f32[256,768]{1,0:T(8,128)}, u32[]{:S(2)}) copy-start(f32[256,768]{1,0:T(8,128)} %copy-done.3) | copy-start | bytes 2359300
  341.0 458.4 %copy-start.11 = (bf16[256,12,64]{0,2,1:T(8,128)(2,1)S(1)}, bf16[256,12,64]{0,2,1:T(8,128)(2,1)}, u32[]{:S(2)}) copy-start(bf16[256,12,64]{0,2,1:T(8,128)(2,1)} %copy-done.10) | copy-start | bytes 1179652
  341.0 458.4 %copy-start.13 = (bf16[256,12,64]{0,2,1:T(8,128)(2,1)S(1)}, bf16[256,12,64]{0,2,1:T(8,128)(2,1)}, u32[]{:S(2)}) copy-start(bf16[256,12,64]{0,2,1:T(8,128)(2,1)} %copy-done.12) | copy-start | bytes 1179652
  341.0 458.4 %copy-start.32 = (bf16[12,64,256]{2,1,0:T(8,128)(2,1)S(1)}, bf16[12,64,256]{2,1,0:T(8,128)(2,1)}, u32[]{:S(2)}) copy-start(bf16[12,64,256]{2,1,0:T(8,128)(2,1)} %copy-done.31) | copy-start | bytes 1179652
  341.0 458.4 %copy-start.57 = (f32[256]{0:T(256)S(1)}, f32[256]{0:T(256)}, u32[]{:S(2)}) copy-start(f32[256]{0:T(256)} %copy-done.56) | copy-start | bytes 3076
  341.1 468.9 %reduce-scatter.17.cloned.1.call-start = ((), (), s32[]{:S(2)}) async-start(), calls=%async_computation.15 | async-start | bytes 110592 | tf_op jit(solution)/shard_map/reduce_scatter | solution.py:289
  358.0 465.5 %reduce-scatter.33.cloned.1.call-start = ((), (), s32[]{:S(2)}) async-start(), calls=%async_computation.23 | async-start | bytes 331776 | tf_op jit(solution)/shard_map/reduce_scatter | solution.py:286
  452.3 386.1 %reduce-scatter.21.cloned.1.call-start = ((), (), s32[]{:S(2)}) async-start(), calls=%async_computation.17 | async-start | bytes 442368 | tf_op jit(solution)/shard_map/reduce_scatter | solution.py:292
  566.9 285.9 %reduce-scatter.25.cloned.1.call-start = ((), (), s32[]{:S(2)}) async-start(), calls=%async_computation.19 | async-start | bytes 442368 | tf_op jit(solution)/shard_map/reduce_scatter | solution.py:295
  682.7 184.3 %reduce-scatter.29.cloned.1.call-start = ((), (), s32[]{:S(2)}) async-start(), calls=%async_computation.21 | async-start | bytes 442368 | tf_op jit(solution)/shard_map/reduce_scatter | solution.py:298
  (38 other events, 49.3 us)
Sparse Core Ops, SparseCore 0:
  10.3 54.1 all-gather.5
  66.8 42.1 all-gather.7
  111.3 54.7 all-gather.9
  168.2 51.8 all-gather.11
  297.2 59.2 reduce-scatter.14
  360.9 89.1 reduce-scatter.30
  454.1 110.8 reduce-scatter.18
  569.7 111.1 reduce-scatter.22
  684.9 112.5 reduce-scatter.26
  800.2 9.6 reduce-scatter.16
  812.3 11.2 reduce-scatter.32
  826.3 12.0 reduce-scatter.20
  840.7 12.0 reduce-scatter.24
  854.9 12.0 reduce-scatter.28
